TPU v7x, 32 devices: a whole 2x2x4 slice. The times are simulated.
32 devices in a mesh: ens: 2 (over y), mem: 4 (over x, core), lon: 4 (over z).
Axes of the slice: x: 2, y: 2, z: 4, core: 2. Of those that a mesh axis runs over, the one named last changes fastest.
Arguments:
- initial_state: float32 [8, 4, 4, 256, 128], P(('ens', 'mem'), None, None, 'lon'), parts along dimension 0, may hold values from -1.25 to 1.25
- ancestor: int32 [8], P(('ens', 'mem')), parts along dimension 0, may hold values from 0 to 3
- selector: int32 [8], P(('ens', 'mem')), parts along dimension 0, may hold values from 0 to 3
- perturbations: float32 [8, 4, 4, 256, 128], P('ens', None, None, 'lon'), parts along dimension 0, may hold values from -0.5 to 0.5
- diffusivity: float32 [4, 256, 128], P(None, 'lon'), may hold values from 0.05 to 0.3
- region_weight: float32 [256, 128], P('lon'), may hold values from 0.3 to 27, as said below
Outputs:
- final_state: float32 [8, 4, 4, 256, 128], P(('ens', 'mem'), None, None, 'lon'), parts along dimension 0
- actions: float32 [8, 2], P(('ens', 'mem')), parts along dimension 0
There are 2 independent parts, one for each index of `ens`. A program takes and returns all parts, laid end to end along the dimension named above; an argument that names none is the same for every part. Nothing has to cross between parts.
Inputs may be any that keep to these rules, and one draw needn't show every extreme that they name: `region_weight`: Positive.
All inputs are finite; a program needn't handle non-finite values.
Results may differ from a plain program's by a relative error of at most 0.0001.
Values sent between devices are 32-bit elements; how exact they have to be, the bound alone decides.
A program may use at most 64 MiB of HBM per device.

v0:
```python
import jax
import jax.numpy as jnp
from jax import lax
from jax.sharding import PartitionSpec as P

LAT = 128
LEV = 4
STEPS = 3


TIME_STEP = 0.2


def with_halo(block, sides, width):
    for axis, dim in sides:
        count = lax.axis_size(axis)
        forward = [(i, i + 1) for i in range(count - 1)]
        forward.append((count - 1, 0))
        backward = [(target, source) for source, target in forward]
        low = lax.ppermute(
            lax.slice_in_dim(block, block.shape[dim] - width, None, axis=dim), axis, forward
        )
        high = lax.ppermute(lax.slice_in_dim(block, 0, width, axis=dim), axis, backward)
        block = jnp.concatenate([low, block, high], axis=dim)
    return block


def shifted_lat(tracer_field, upward_flux):
    if upward_flux:
        return jnp.concatenate([tracer_field[..., 1:], tracer_field[..., -1:]], axis=-1)
    return jnp.concatenate([tracer_field[..., :1], tracer_field[..., :-1]], axis=-1)


def advance(padded, kappa_pad):
    centre = padded[..., 1:-1, :]
    west_cell = padded[..., :-2, :]
    east_cell = padded[..., 2:, :]
    south_cell = shifted_lat(centre, False)
    north_cell = shifted_lat(centre, True)
    kappa_mid = kappa_pad[..., 1:-1, :]
    kappa_west = 0.5 * (kappa_mid + kappa_pad[..., :-2, :])
    kappa_east = 0.5 * (kappa_mid + kappa_pad[..., 2:, :])
    kappa_south = 0.5 * (kappa_mid + shifted_lat(kappa_mid, False))
    kappa_north = 0.5 * (kappa_mid + shifted_lat(kappa_mid, True))
    zonal_wind = centre[:, 0:1]
    merid_wind = centre[:, 1:2]
    transport = (
        jnp.maximum(zonal_wind, 0.0) * (centre - west_cell)
        + jnp.minimum(zonal_wind, 0.0) * (east_cell - centre)
        + jnp.maximum(merid_wind, 0.0) * (centre - south_cell)
        + jnp.minimum(merid_wind, 0.0) * (north_cell - centre)
    )
    mixing = (
        kappa_east * (east_cell - centre)
        - kappa_west * (centre - west_cell)
        + kappa_north * (north_cell - centre)
        - kappa_south * (centre - south_cell)
    )
    return centre + TIME_STEP * (mixing - transport)


def measure(tracer_field, clone_weight):
    thermal_field = tracer_field[:, 2]
    return jnp.sum(clone_weight * thermal_field * thermal_field, axis=(1, 2, 3))


def body(initial_state, ancestor, selector, perturbations, diffusivity, region_weight):
    cell_count = LEV * LAT * initial_state.shape[3] * lax.axis_size("lon")
    kappa_pad = with_halo(diffusivity, (("lon", 1),), STEPS)

    def integrate_block(present_state):
        partial_value = []
        padded = with_halo(present_state, (("lon", 3),), STEPS)
        for section in range(STEPS):
            width_now = kappa_pad.shape[1] - 2 * section
            padded = advance(
                padded, lax.slice_in_dim(kappa_pad, section, section + width_now, axis=1)
            )
            margin = STEPS - 1 - section
            partial_value.append(
                measure(padded[..., margin : padded.shape[3] - margin, :], region_weight)
            )
        present_state = padded
        running = jnp.zeros((present_state.shape[0],), jnp.float32)
        for part_sum in partial_value:
            running = running + lax.psum(part_sum, "lon") / cell_count
        return (present_state, running)

    added = jnp.take(perturbations, selector, axis=0)
    middle, first_action = integrate_block(initial_state)
    shard_rows = lax.all_gather(middle, "mem", axis=0, tiled=True)
    row_count = shard_rows.shape[0]
    inside = (ancestor >= 0) & (ancestor < row_count)
    chosen = jnp.take(shard_rows, jnp.clip(ancestor, 0, row_count - 1), axis=0)
    ancestry = jnp.where(inside[:, None, None, None, None], chosen, jnp.zeros_like(middle))
    cloned = ancestry + added
    final_state, second_action = integrate_block(cloned)
    return (final_state, jnp.stack([first_action, second_action], axis=1))


def solution(mesh):
    in_specs = (
        P(("ens", "mem"), None, None, "lon", None),
        P(("ens", "mem")),
        P(("ens", "mem")),
        P("ens", None, None, "lon", None),
        P(None, "lon", None),
        P("lon", None),
    )
    out_specs = (P(("ens", "mem"), None, None, "lon", None), P(("ens", "mem"), None))
    return jax.shard_map(body, mesh=mesh, in_specs=in_specs, out_specs=out_specs, check_vma=False)
```

profile of v0, /device:TPU:0, one launch (start us, length us, event | category | flops | bytes accessed | tf_op | source)
XLA Modules:
  0.0 88.0 jit_solution(6995215156166214650)
XLA Ops:
  7.2 0.0 all-gather.2.cloned.1.call-start
  7.2 0.8 fusion.39
  8.0 3.1 %collective-permute-start.2 = (f32[4,3,128]{2,1,0:T(4,128)S(1)}, f32[4,3,128]{2,1,0:T(4,128)S(1)}, u32[]{:S(2)}, u32[]{:S(2)}) collective-permute-start(f32[4,3,128]{2,1,0:T(4,128)S(1)} %get-tuple-element.98), channel_id=1, source_target_pairs={{0,1},{1,2},{2,3},{3,0},{4,5},{5,6},{6,7},{7,4},{8,9},{9,10},{10,1... | collective-permute-start | bytes 18440 | tf_op jit(solution)/shard_map/ppermute | solution.py:20
  11.0 2.1 %collective-permute-start.3 = (f32[4,3,128]{2,1,0:T(4,128)S(1)}, f32[4,3,128]{2,1,0:T(4,128)S(1)}, u32[]{:S(2)}, u32[]{:S(2)}) collective-permute-start(f32[4,3,128]{2,1,0:T(4,128)S(1)} %get-tuple-element.99), channel_id=1, source_target_pairs={{1,0},{2,1},{3,2},{0,3},{5,4},{6,5},{7,6},{4,7},{9,8},{10,9},{11,1... | collective-permute-start | bytes 18440 | tf_op jit(solution)/shard_map/ppermute | solution.py:23
  13.1 0.9 %fusion.32 = (f32[1,4,4,3,128]{4,3,2,1,0:T(4,128)S(1)}, f32[1,4,4,3,128]{4,3,2,1,0:T(4,128)S(1)}) fusion(f32[1,4,4,64,128]{4,3,2,1,0:T(8,128)} %param.8), kind=kLoop, calls=%fused_computation.118 | loop fusion | bytes 98304 | tf_op jit(solution)/shard_map/slice | solution.py:21
  14.0 0.1 collective-permute-start
  14.1 3.8 %collective-permute-start.1 = (f32[1,4,4,3,128]{4,3,2,1,0:T(4,128)S(1)}, f32[1,4,4,3,128]{4,3,2,1,0:T(4,128)S(1)}, u32[]{:S(2)}, u32[]{:S(2)}) collective-permute-start(f32[1,4,4,3,128]{4,3,2,1,0:T(4,128)S(1)} %get-tuple-element.73), channel_id=1, source_target_pairs={{1,0},{2,1},{3,2},{0,3},{5,4},{6,5},{7,6},{4,7},{9,8},{10,9},{11,1... | collective-permute-start | bytes 73736 | tf_op jit(solution)/shard_map/ppermute | solution.py:23
  17.9 1.1 %fusion.38 = (f32[4,64,1]{2,1,0:T(8,128)S(1)}, f32[4,64,1]{2,1,0:T(8,128)S(1)}) fusion(f32[4,64,128]{2,1,0:T(8,128)} %param.12), kind=kLoop, calls=%fused_computation.124 | loop fusion | bytes 4096 | tf_op jit(solution)/shard_map/slice | solution.py:30
  19.0 1.1 %fusion.37 = (f32[4,64,127]{2,1,0:T(8,128)S(1)}, f32[4,64,127]{2,1,0:T(8,128)S(1)}) fusion(f32[4,64,128]{2,1,0:T(8,128)} %param.12), kind=kLoop, calls=%fused_computation.123 | loop fusion | bytes 520192 | tf_op jit(solution)/shard_map/slice | solution.py:30
  20.0 0.9 %constant_dynamic-update-slice_fusion.1 = f32[4,67,128]{2,1,0:T(8,128)S(1)} fusion(f32[4,64,128]{2,1,0:T(8,128)} %param.12), kind=kLoop, calls=%fused_computation.103 | loop fusion | bytes 262144
  21.0 0.9 %pad_maximum_fusion.2 = f32[4,70,128]{2,1,0:T(8,128)S(1)} fusion(f32[4,3,128]{2,1,0:T(4,128)S(1)} %collective-permute-done.3, f32[4,64,128]{2,1,0:T(8,128)} %param.12, f32[4,3,128]{2,1,0:T(4,128)S(1)} %collective-permute-done.2), kind=kLoop, calls=%fused_computation.48 | loop fusion | flops 71680 | bytes 286720 | tf_op jit(solution)/shard_map/concatenate | solution.py:24
  21.9 0.1 fusion.36
  22.0 0.1 fusion.35
  22.1 0.1 fusion.34
  22.2 0.1 fusion.33
  22.4 0.1 fusion.16
  22.5 0.2 fusion.1
  22.7 0.2 fusion.3
  22.9 0.6 copy-done.2
  23.4 0.1 pad_maximum_fusion
  23.5 0.2 fusion.29
  23.8 0.2 fusion.30
  24.0 0.7 multiply_add_fusion.3
  24.7 0.2 fusion.28
  25.0 0.2 fusion.27
  25.2 0.7 multiply_add_fusion.2
  25.9 0.2 fusion.26
  26.2 0.2 fusion.25
  26.4 1.4 %multiply_add_fusion.5 = f32[1,4,4,64,128]{4,3,2,1,0:T(8,128)} fusion(f32[1,4,4,64,127]{4,3,2,1,0:T(8,128)S(1)} %get-tuple-element.51, f32[1,4,4,64,1]{4,3,2,1,0:T(8,128)S(1)} %get-tuple-element.53, f32[1,4,4,64,1]{4,3,2,1,0:T(8,128)S(1)} %get-tuple-element.52, f32[1,4,4,64,127]{4,3,2,1,0:T(8,128)S(1)} %get-tuple-element.50, ...), kind=kLoop, calls=%fused_computation.33 | loop fusion | flops 3014656 | bytes 4194304 | tf_op jit(solution)/shard_map/add | solution.py:59
  29.1 19.8 %all-gather.2.cloned.1.call-done = f32[4,4,4,64,128]{4,3,2,1,0:T(8,128)} async-done(((f32[1,4,4,64,128]{4,3,2,1,0:T(8,128)}), f32[4,4,4,64,128]{4,3,2,1,0:T(8,128)}) %all-gather.2.cloned.1.call-update) | async-done | bytes 2097168 | tf_op jit(solution)/shard_map/all_gather | solution.py:91
  48.9 1.3 %select_add_fusion = f32[1,4,4,64,128]{4,3,2,1,0:T(8,128)S(1)} fusion(f32[4,4,4,64,128]{4,3,2,1,0:T(8,128)} %param.11, s32[]{:T(128)} %bitcast.16, f32[4,4,4,64,128]{4,3,2,1,0:T(8,128)} %all-gather.2.cloned.1.call-done, s32[]{:T(128)} %bitcast.14, pred[]{:T(512)} %bitcast.15, pred[]{:T(512)} %bitcast.1, pred[]{:T(512)} %bitcast), kind=kLoop, calls=%fused_computation.30 | loop fusion | flops 524288 | bytes 1572875 | tf_op jit(solution)/shard_map/add | solution.py:96
  50.2 1.5 %collective-permute-start.4 = (f32[1,4,4,3,128]{4,3,2,1,0:T(4,128)S(1)}, f32[1,4,4,3,128]{4,3,2,1,0:T(4,128)S(1)}, u32[]{:S(2)}, u32[]{:S(2)}) collective-permute-start(f32[1,4,4,3,128]{4,3,2,1,0:T(4,128)S(1)} %get-tuple-element.70), channel_id=1, source_target_pairs={{0,1},{1,2},{2,3},{3,0},{4,5},{5,6},{6,7},{7,4},{8,9},{9,10},{10,1... | collective-permute-start | bytes 73736 | tf_op jit(solution)/shard_map/ppermute | solution.py:20
  51.8 2.3 %collective-permute-start.5 = (f32[1,4,4,3,128]{4,3,2,1,0:T(4,128)S(1)}, f32[1,4,4,3,128]{4,3,2,1,0:T(4,128)S(1)}, u32[]{:S(2)}, u32[]{:S(2)}) collective-permute-start(f32[1,4,4,3,128]{4,3,2,1,0:T(4,128)S(1)} %get-tuple-element.71), channel_id=1, source_target_pairs={{1,0},{2,1},{3,2},{0,3},{5,4},{6,5},{7,6},{4,7},{9,8},{10,9},{11,1... | collective-permute-start | bytes 73736 | tf_op jit(solution)/shard_map/ppermute | solution.py:23
  54.1 1.9 %collective-permute-done.4 = f32[1,4,4,3,128]{4,3,2,1,0:T(4,128)S(1)} collective-permute-done((f32[1,4,4,3,128]{4,3,2,1,0:T(4,128)S(1)}, f32[1,4,4,3,128]{4,3,2,1,0:T(4,128)S(1)}, u32[]{:S(2)}, u32[]{:S(2)}) %collective-permute-start.4) | collective-permute-done | bytes 24608 | tf_op jit(solution)/shard_map/ppermute | solution.py:20
  56.0 0.1 pad_maximum_fusion.1
  56.2 0.2 fusion.23
  56.4 0.2 fusion.24
  56.6 0.7 multiply_add_fusion.1
  57.4 0.2 fusion.22
  57.6 0.2 fusion.21
  57.8 0.7 multiply_add_fusion
  58.5 0.2 fusion.20
  58.8 0.2 fusion.19
  59.0 0.6 multiply_add_fusion.4
  59.6 0.1 copy-done.3
  59.8 1.8 %fusion.10 = (f32[]{:T(128)}, f32[]{:T(128)}, f32[]{:T(128)}, f32[]{:T(128)}, f32[]{:T(128)}, /*index=5*/f32[]{:T(128)}) fusion(f32[1,4,4,64,128]{4,3,2,1,0:T(8,128)} %multiply_add_fusion.5, f32[64,128]{1,0:T(8,128)S(1)} %copy-done.3, f32[1,4,4,66,128]{4,3,2,1,0:T(8,128)S(1)} %multiply_add_fusion.2, f32[1,4,4,68,128]{4,3,2,1,0:T(8,128)S(1)} %multiply_add_fusion.1, ...), kind=kLoop, calls=%fused_computation.75 | loop fusion | flops 589818 | bytes 819224 | tf_op jit(solution)/shard_map/reduce_sum | solution.py:64
  65.5 13.8 %all-reduce = (f32[1]{0:T(128)}, f32[1]{0:T(128)}) all-reduce(f32[1]{0:T(128)} %bitcast.37, f32[1]{0:T(128)} %bitcast.32), channel_id=1, replica_groups=mesh['ens'=2,'mem'=4,'lon'=4] {'lon'}, use_global_device_ids=true, to_apply=%region_7.9 | all-reduce | flops 2 | bytes 16 | tf_op jit(solution)/shard_map/psum | solution.py:86
  80.5 0.6 pad_maximum_fusion.4
  (20 shorter events, 0.3 us)
Async XLA Ops:
  7.2 15.2 %copy-start = (f32[4,64,128]{2,1,0:T(8,128)S(1)}, f32[4,64,128]{2,1,0:T(8,128)}, u32[]{:S(2)}) copy-start(f32[4,64,128]{2,1,0:T(8,128)} %param.12) | copy-start | bytes 393220
  7.2 41.8 %all-gather.2.cloned.1.call-start = ((), (), s32[]{:S(2)}) async-start(), calls=%async_computation | async-start | bytes 2621440 | tf_op jit(solution)/shard_map/all_gather | solution.py:91
  8.0 13.0 %collective-permute-start.2 = (f32[4,3,128]{2,1,0:T(4,128)S(1)}, f32[4,3,128]{2,1,0:T(4,128)S(1)}, u32[]{:S(2)}, u32[]{:S(2)}) collective-permute-start(f32[4,3,128]{2,1,0:T(4,128)S(1)} %get-tuple-element.98), channel_id=1, source_target_pairs={{0,1},{1,2},{2,3},{3,0},{4,5},{5,6},{6,7},{7,4},{8,9},{9,10},{10,1... | collective-permute-start | bytes 18440 | tf_op jit(solution)/shard_map/ppermute | solution.py:20
  11.0 9.9 %collective-permute-start.3 = (f32[4,3,128]{2,1,0:T(4,128)S(1)}, f32[4,3,128]{2,1,0:T(4,128)S(1)}, u32[]{:S(2)}, u32[]{:S(2)}) collective-permute-start(f32[4,3,128]{2,1,0:T(4,128)S(1)} %get-tuple-element.99), channel_id=1, source_target_pairs={{1,0},{2,1},{3,2},{0,3},{5,4},{6,5},{7,6},{4,7},{9,8},{10,9},{11,1... | collective-permute-start | bytes 18440 | tf_op jit(solution)/shard_map/ppermute | solution.py:23
  14.0 8.8 %collective-permute-start = (f32[1,4,4,3,128]{4,3,2,1,0:T(4,128)S(1)}, f32[1,4,4,3,128]{4,3,2,1,0:T(4,128)S(1)}, u32[]{:S(2)}, u32[]{:S(2)}) collective-permute-start(f32[1,4,4,3,128]{4,3,2,1,0:T(4,128)S(1)} %get-tuple-element.72), channel_id=1, source_target_pairs={{0,1},{1,2},{2,3},{3,0},{4,5},{5,6},{6,7},{7,4},{8,9},{9,10},{10,1... | collective-permute-start | bytes 73736 | tf_op jit(solution)/shard_map/ppermute | solution.py:20
  14.1 8.8 %collective-permute-start.1 = (f32[1,4,4,3,128]{4,3,2,1,0:T(4,128)S(1)}, f32[1,4,4,3,128]{4,3,2,1,0:T(4,128)S(1)}, u32[]{:S(2)}, u32[]{:S(2)}) collective-permute-start(f32[1,4,4,3,128]{4,3,2,1,0:T(4,128)S(1)} %get-tuple-element.73), channel_id=1, source_target_pairs={{1,0},{2,1},{3,2},{0,3},{5,4},{6,5},{7,6},{4,7},{9,8},{10,9},{11,1... | collective-permute-start | bytes 73736 | tf_op jit(solution)/shard_map/ppermute | solution.py:23
  22.4 1.0 %copy-start.2 = (f32[1,4,4,64,128]{4,3,2,1,0:T(8,128)S(1)}, f32[1,4,4,64,128]{4,3,2,1,0:T(8,128)}, u32[]{:S(2)}) copy-start(f32[1,4,4,64,128]{4,3,2,1,0:T(8,128)} %param.8) | copy-start | bytes 1572868
  50.2 5.8 %collective-permute-start.4 = (f32[1,4,4,3,128]{4,3,2,1,0:T(4,128)S(1)}, f32[1,4,4,3,128]{4,3,2,1,0:T(4,128)S(1)}, u32[]{:S(2)}, u32[]{:S(2)}) collective-permute-start(f32[1,4,4,3,128]{4,3,2,1,0:T(4,128)S(1)} %get-tuple-element.70), channel_id=1, source_target_pairs={{0,1},{1,2},{2,3},{3,0},{4,5},{5,6},{6,7},{7,4},{8,9},{9,10},{10,1... | collective-permute-start | bytes 73736 | tf_op jit(solution)/shard_map/ppermute | solution.py:20
  51.8 4.3 %collective-permute-start.5 = (f32[1,4,4,3,128]{4,3,2,1,0:T(4,128)S(1)}, f32[1,4,4,3,128]{4,3,2,1,0:T(4,128)S(1)}, u32[]{:S(2)}, u32[]{:S(2)}) collective-permute-start(f32[1,4,4,3,128]{4,3,2,1,0:T(4,128)S(1)} %get-tuple-element.71), channel_id=1, source_target_pairs={{1,0},{2,1},{3,2},{0,3},{5,4},{6,5},{7,6},{4,7},{9,8},{10,9},{11,1... | collective-permute-start | bytes 73736 | tf_op jit(solution)/shard_map/ppermute | solution.py:23
  59.0 0.8 copy-start.3
  59.7 21.4 %copy-start.1 = (f32[1,4,4,64,128]{4,3,2,1,0:T(8,128)}, f32[1,4,4,64,128]{4,3,2,1,0:T(8,128)S(1)}, u32[]{:S(2)}) copy-start(f32[1,4,4,64,128]{4,3,2,1,0:T(8,128)S(1)} %multiply_add_fusion.4) | copy-start | bytes 1572868
Sparse Core Ops, SparseCore 0:
  28.0 20.9 all-gather.1
where the time goes:
time: 88.5 us; the launch traced here: 88 us
  waiting for transfers between devices  21.7 us (25%)
  between operations  20.8 us (24%)
  blocking collectives  13.8 us (16%)
  starting transfers between devices  12.9 us (15%)
  other arithmetic  10.2 us (12%)
  local copies, waits for them, and re-layouts  8.49 us (10%)
    all_gather x1, waiting for transfers between devices, body(): shard_rows = lax.all_gather(middle, 'mem', axis=0, tiled=True)  19.8 us
    psum x1, blocking collectives, integrate_block(): running = running + lax.psum(part_sum, 'lon') / cell_count  13.8 us
    ppermute x3, starting transfers between devices, with_halo(): lax.ppermute(lax.slice_in_dim(block, 0, width, axis=dim), axis, backward)  8.22 us
    add x6, other arithmetic, advance(): return centre + TIME_STEP * (mixing - transport)  4.78 us
    ppermute x3, starting transfers between devices, with_halo(): lax.ppermute(lax.slice_in_dim(block, block.shape[dim] - width, None, axis...  4.65 us
    slice x9, local copies, waits for them, and re-layouts, shifted_lat(): tracer_field[..., 1:]  2.6 us
    slice x9, local copies, waits for them, and re-layouts, shifted_lat(): tracer_field[..., -1:]  2.6 us
    ppermute x3, waiting for transfers between devices, with_halo(): lax.ppermute(lax.slice_in_dim(block, block.shape[dim] - width, None, axis...  1.93 us
  transfers between devices with their start and end apart: 7, of which 2 were waited for; matrix products, arithmetic and copies ran while one was open for 7% of the time, Pallas kernels for 0%

commit v1 on v0

v1 whole, which is shorter than its diff:
```python
import functools

import jax
import jax.numpy as jnp
from jax import lax
from jax.experimental import pallas as pl
from jax.experimental.pallas import tpu as pltpu
from jax.sharding import PartitionSpec as P

STEPS = 3
TIME_STEP = 0.2
EDGE = 8
MESH_ID = pl.DeviceIdType.MESH


def kernel(
    n, ring, anc_ref, sel_ref, init_ref, pert_ref, kap_ref, weight_ref, out_ref, act_ref,
    full, state, own, pert, pert_edge, pert_halo, edge, kap, face, coef, weight, part,
    x_send, x_recv, p_send, p_recv, z_send, z_recv, s_send, s_recv, local_sem,
):
    _, fields, levels, width, lat = init_ref.shape
    rows = width + 2 * EDGE
    dyn = fields - 1
    groups = n // 2
    mem = lax.axis_index("mem")
    lon = lax.axis_index("lon")
    twin = mem + 1 - 2 * lax.rem(mem, 2)
    east, west = lax.rem(lon + 1, ring), lax.rem(lon + ring - 1, ring)
    top = width - EDGE

    local = [
        pltpu.make_async_copy(init_ref.at[0], full.at[mem], local_sem.at[0]),
        pltpu.make_async_copy(
            init_ref.at[0, pl.ds(0, dyn)], own.at[:, :, pl.ds(EDGE, width)], local_sem.at[1]
        ),
        pltpu.make_async_copy(kap_ref, kap.at[:, pl.ds(EDGE, width)], local_sem.at[2]),
        pltpu.make_async_copy(weight_ref, weight, local_sem.at[3]),
        pltpu.make_async_copy(pert_ref, pert, local_sem.at[4]),
    ]
    for copy in local:
        copy.start()

    barrier = pltpu.get_barrier_semaphore()
    peers = 0
    for k in range(1, groups):
        pl.semaphore_signal(
            barrier, inc=1, device_id={"mem": lax.rem(mem + 2 * k, n)}, device_id_type=MESH_ID
        )
        peers += 1
    pl.semaphore_signal(barrier, inc=1, device_id={"mem": twin}, device_id_type=MESH_ID)
    peers += 1
    for d in range(1, ring):
        pl.semaphore_signal(
            barrier, inc=1, device_id={"lon": lax.rem(lon + d, ring)}, device_id_type=MESH_ID
        )
        peers += 1
    pl.semaphore_wait(barrier, peers)

    def view(block, kind, level):
        if kind == "lo":
            return block.at[:, :, pl.ds(0, EDGE)]
        if kind == "hi":
            return block.at[:, :, pl.ds(top, EDGE)]
        if kind == "dyn":
            return block.at[pl.ds(0, dyn), level, pl.ds(EDGE, width - 2 * EDGE)]
        return block.at[dyn, level, pl.ds(EDGE, width - 2 * EDGE)]

    def sem_of(kind, level):
        return {"lo": 0, "hi": 1, "dyn": 2 + level, "hum": 2 + levels + level}[kind]

    def across(k, kind, level):
        slot = sem_of(kind, level)
        return pltpu.make_async_remote_copy(
            src_ref=view(init_ref.at[0], kind, level),
            dst_ref=view(full.at[mem], kind, level),
            send_sem=x_send.at[k - 1, slot],
            recv_sem=x_recv.at[k - 1, slot],
            device_id={"mem": lax.rem(mem + 2 * k, n)},
            device_id_type=MESH_ID,
        )

    def to_twin(k, kind, level):
        slot = sem_of(kind, level)
        member = lax.rem(mem + n - 2 * k, n)
        source = init_ref.at[0] if k == 0 else full.at[member]
        return pltpu.make_async_remote_copy(
            src_ref=view(source, kind, level),
            dst_ref=view(full.at[member], kind, level),
            send_sem=p_send.at[k, slot],
            recv_sem=p_recv.at[k, slot],
            device_id={"mem": twin},
            device_id_type=MESH_ID,
        )

    def lon_copy(source, target, slot, side):
        return pltpu.make_async_remote_copy(
            src_ref=source,
            dst_ref=target,
            send_sem=z_send.at[slot, side],
            recv_sem=z_recv.at[slot, side],
            device_id={"lon": east if side else west},
            device_id_type=MESH_ID,
        )

    low, high = pl.ds(0, EDGE), pl.ds(EDGE + width, EDGE)
    first, last = pl.ds(0, EDGE), pl.ds(top, EDGE)
    pieces = [("lo", 0), ("hi", 0)]
    pieces += [("dyn", level) for level in range(levels)]
    pieces += [("hum", level) for level in range(levels)]
    for kind, level in pieces:
        for k in range(1, groups):
            across(k, kind, level).start()
    own_halo = [
        lon_copy(init_ref.at[0, pl.ds(0, dyn), :, first], own.at[:, :, high], 0, 0),
        lon_copy(init_ref.at[0, pl.ds(0, dyn), :, last], own.at[:, :, low], 0, 1),
    ]
    kap_halo = [
        lon_copy(kap_ref.at[:, first], kap.at[:, high], 1, 0),
        lon_copy(kap_ref.at[:, last], kap.at[:, low], 1, 1),
    ]
    for copy in kap_halo + own_halo:
        copy.start()
    for kind, level in pieces:
        to_twin(0, kind, level).start()

    local[4].wait()
    chosen = sel_ref[0]
    for f in range(fields):
        for level in range(levels):
            pert_edge[0, f, level] = pert[chosen, f, level, 0:EDGE, :]
            pert_edge[1, f, level] = pert[chosen, f, level, top:width, :]
    pert_copy = [
        lon_copy(pert_edge.at[0], pert_halo.at[1], 2, 0),
        lon_copy(pert_edge.at[1], pert_halo.at[0], 2, 1),
    ]
    for copy in pert_copy:
        copy.start()

    for copy in local[:4]:
        copy.wait()
    for copy in kap_halo:
        copy.wait()

    lane = lax.broadcasted_iota(jnp.int32, (rows, lat), 1)
    not_north = jnp.where(lane == lat - 1, 0.0, 1.0)
    not_south = jnp.where(lane == 0, 0.0, 1.0)

    def from_west(q):
        return pltpu.roll(q, 1, 0)

    def from_east(q):
        return pltpu.roll(q, rows - 1, 0)

    def from_south(q):
        return pltpu.roll(q, 1, 1)

    def from_north(q):
        return pltpu.roll(q, lat - 1, 1)

    def faces(level, _):
        k = kap[level]
        to_east = (0.5 * TIME_STEP) * (k + from_east(k))
        to_north = (0.5 * TIME_STEP) * (k + from_north(k)) * not_north
        face[0, level] = to_east
        face[1, level] = from_west(to_east)
        face[2, level] = to_north
        face[3, level] = from_south(to_north)
        return 0

    lax.fori_loop(0, levels, faces, 0)

    def coefficients(u, v, level):
        u = TIME_STEP * u
        v = TIME_STEP * v
        to_e = face[0, level] - jnp.minimum(u, 0.0)
        to_w = face[1, level] + jnp.maximum(u, 0.0)
        to_n = face[2, level] - jnp.minimum(v, 0.0) * not_north
        to_s = face[3, level] + jnp.maximum(v, 0.0) * not_south
        here = 1.0 - ((to_e + to_w) + (to_n + to_s))
        return to_e, to_w, to_n, to_s, here

    def moved(q, c):
        to_e, to_w, to_n, to_s, here = c
        return (
            here * q
            + (to_e * from_east(q) + to_w * from_west(q))
            + (to_n * from_north(q) + to_s * from_south(q))
        )

    def observed(t):
        inner = t[EDGE : EDGE + width, :]
        terms = weight[...] * inner * inner
        return jnp.sum(terms.reshape(width // 8, 8, lat), axis=0)

    for copy in own_halo:
        copy.wait()

    def own_level(level, total):
        u, v, t = own[0, level], own[1, level], own[2, level]
        for step in range(STEPS):
            c = coefficients(u, v, level)
            t_next = moved(t, c)
            if step < STEPS - 1:
                u, v = moved(u, c), moved(v, c)
            t = t_next
            total = total + observed(t)
        return total

    part[0, lon] = lax.fori_loop(0, levels, own_level, jnp.zeros((8, lat), jnp.float32))

    def share(which):
        return [
            pltpu.make_async_remote_copy(
                src_ref=part.at[which, lon],
                dst_ref=part.at[which, lon],
                send_sem=s_send.at[which, d - 1],
                recv_sem=s_recv.at[which, d - 1],
                device_id={"lon": lax.rem(lon + d, ring)},
                device_id_type=MESH_ID,
            )
            for d in range(1, ring)
        ]

    def arrive(kind, level):
        for k in range(1, groups):
            across(k, kind, level).wait_recv()
            to_twin(k, kind, level).start()

    def settled(kind, level):
        for k in range(groups):
            to_twin(k, kind, level).wait_recv()

    arrive("lo", 0)
    arrive("hi", 0)
    first_share = share(0)
    for copy in first_share:
        copy.start()
    settled("lo", 0)
    settled("hi", 0)
    ancestor = anc_ref[0]

    def pick(load):
        value = load(0)
        for j in range(1, n):
            value = jnp.where(ancestor == j, load(j), value)
        return value

    for f in range(fields):
        for level in range(levels):
            lower = pick(lambda j: full[j, f, level, 0:EDGE, :])
            upper = pick(lambda j: full[j, f, level, top:width, :])
            edge[0, f, level] = lower
            edge[1, f, level] = upper
            state[f, level, EDGE : 2 * EDGE, :] = lower
            state[f, level, width : width + EDGE, :] = upper
    edge_copy = [
        lon_copy(edge.at[0], state.at[:, :, high], 3, 0),
        lon_copy(edge.at[1], state.at[:, :, low], 3, 1),
    ]
    for copy in edge_copy:
        copy.start()
    arrive("dyn", 0)
    for copy in pert_copy + edge_copy:
        copy.wait()

    def fill(f, level):
        state[f, level, 2 * EDGE : width, :] = pick(
            lambda j: full[j, f, level, EDGE : width - EDGE, :]
        )
        return state[f, level]

    def noise(f, level):
        return jnp.concatenate(
            [pert_halo[0, f, level], pert[chosen, f, level], pert_halo[1, f, level]], axis=0
        )

    def dyn_level(level, total):
        @pl.when(level < levels - 1)
        def _():
            arrive("dyn", level + 1)

        @pl.when(level == levels - 1)
        def _():
            arrive("hum", 0)

        settled("dyn", level)
        u, v, t = fill(0, level), fill(1, level), fill(2, level)
        for step in range(2 * STEPS):
            if step == STEPS:
                u, v, t = u + noise(0, level), v + noise(1, level), t + noise(2, level)
            c = coefficients(u, v, level)
            for i in range(5):
                coef[level, step, i] = c[i]
            u, v, t = moved(u, c), moved(v, c), moved(t, c)
            if step >= STEPS:
                total = total + observed(t)
        inner = slice(EDGE, EDGE + width)
        out_ref[0, 0, level] = u[inner]
        out_ref[0, 1, level] = v[inner]
        out_ref[0, 2, level] = t[inner]
        return total

    part[1, lon] = lax.fori_loop(0, levels, dyn_level, jnp.zeros((8, lat), jnp.float32))
    second_share = share(1)
    for copy in second_share:
        copy.start()

    def hum_level(level, carry):
        @pl.when(level < levels - 1)
        def _():
            arrive("hum", level + 1)

        settled("hum", level)
        q = fill(dyn, level)
        for step in range(2 * STEPS):
            if step == STEPS:
                q = q + noise(dyn, level)
            q = moved(q, [coef[level, step, i] for i in range(5)])
        out_ref[0, dyn, level] = q[EDGE : EDGE + width]
        return carry

    lax.fori_loop(0, levels, hum_level, 0)

    cells = levels * lat * width * ring
    for which, copies in enumerate((first_share, second_share)):
        for copy in copies:
            copy.wait()
        act_ref[0, which] = jnp.sum(jnp.sum(part[which], axis=0)) / cells
    for kind, level in pieces:
        for k in range(1, groups):
            across(k, kind, level).wait_send()
        for k in range(groups):
            to_twin(k, kind, level).wait_send()


def body(initial_state, ancestor, selector, perturbations, diffusivity, region_weight):
    n, ring = lax.axis_size("mem"), lax.axis_size("lon")
    _, fields, levels, width, lat = initial_state.shape
    rows = width + 2 * EDGE
    kinds = 2 + 2 * levels
    f32 = jnp.float32
    any_space = pl.BlockSpec(memory_space=pl.ANY)
    smem = pl.BlockSpec(memory_space=pltpu.SMEM)
    dma = pltpu.SemaphoreType.DMA
    return pl.pallas_call(
        functools.partial(kernel, n, ring),
        out_shape=(
            jax.ShapeDtypeStruct(initial_state.shape, f32),
            jax.ShapeDtypeStruct((1, 2), f32),
        ),
        in_specs=[smem, smem, any_space, any_space, any_space, any_space],
        out_specs=(pl.BlockSpec(memory_space=pltpu.VMEM), smem),
        scratch_shapes=[
            pltpu.VMEM((n, fields, levels, width, lat), f32),
            pltpu.VMEM((fields, levels, rows, lat), f32),
            pltpu.VMEM((fields - 1, levels, rows, lat), f32),
            pltpu.VMEM(perturbations.shape, f32),
            pltpu.VMEM((2, fields, levels, EDGE, lat), f32),
            pltpu.VMEM((2, fields, levels, EDGE, lat), f32),
            pltpu.VMEM((2, fields, levels, EDGE, lat), f32),
            pltpu.VMEM((levels, rows, lat), f32),
            pltpu.VMEM((4, levels, rows, lat), f32),
            pltpu.VMEM((levels, 2 * STEPS, 5, rows, lat), f32),
            pltpu.VMEM((width, lat), f32),
            pltpu.VMEM((2, ring, 8, lat), f32),
            dma((n // 2 - 1, kinds)),
            dma((n // 2 - 1, kinds)),
            dma((n // 2, kinds)),
            dma((n // 2, kinds)),
            dma((4, 2)),
            dma((4, 2)),
            dma((2, ring - 1)),
            dma((2, ring - 1)),
            dma((5,)),
        ],
        compiler_params=pltpu.CompilerParams(
            collective_id=0, has_side_effects=True, vmem_limit_bytes=40 * 1024 * 1024
        ),
    )(ancestor, selector, initial_state, perturbations, diffusivity, region_weight)


def solution(mesh):
    in_specs = (
        P(("ens", "mem"), None, None, "lon", None),
        P(("ens", "mem")),
        P(("ens", "mem")),
        P("ens", None, None, "lon", None),
        P(None, "lon", None),
        P("lon", None),
    )
    out_specs = (P(("ens", "mem"), None, None, "lon", None), P(("ens", "mem"), None))
    return jax.shard_map(body, mesh=mesh, in_specs=in_specs, out_specs=out_specs, check_vma=False)
```

time: 88.5 us -> 33.4 us (0.38)
  Pallas kernels: 0 us -> 25.6 us
  waiting for transfers between devices: 21.7 us -> 0 us
  between operations: 20.8 us -> 1.94 us
  blocking collectives: 13.8 us -> 0 us
  starting transfers between devices: 12.9 us -> 0 us
  other arithmetic: 10.2 us -> 0 us
  local copies, waits for them, and re-layouts: 8.49 us -> 5.59 us
    pallas_call x0 -> x1, Pallas kernels: none -> 25.6 us  [body(): pl.pallas_call(functools.partial(kernel, n, ring), out_shape=(jax.ShapeDt...]
    all_gather x1 -> x0, waiting for transfers between devices: 19.8 us -> none  [body(): shard_rows = lax.all_gather(middle, 'mem', axis=0, tiled=True)]
    psum x1 -> x0, blocking collectives: 13.8 us -> none  [integrate_block(): running = running + lax.psum(part_sum, 'lon') / cell_count]
    ppermute x6 -> x0, starting transfers between devices: 12.9 us -> none  [the longest x3 8.22 us: with_halo(): lax.ppermute(lax.slice_in_dim(block, 0, width, axis=dim), axis, backward)]
    slice x21 -> x0, local copies, waits for them, and re-layouts: 6.87 us -> none  [the longest x9 2.6 us: shifted_lat(): tracer_field[..., 1:]]
    add x7 -> x0, other arithmetic: 6.06 us -> none  [the longest x6 4.78 us: advance(): return centre + TIME_STEP * (mixing - transport)]
    unnamed x9 -> x10, local copies, waits for them, and re-layouts: 1.61 us -> 5.59 us
    ppermute x6 -> x0, waiting for transfers between devices: 1.94 us -> none  [the longest x3 1.93 us: with_halo(): lax.ppermute(lax.slice_in_dim(block, block.shape[dim] - width, None, axis...]
  transfers between devices with their start and end apart: 7 -> 0, of which waited for: 2 -> 0; matrix products, arithmetic and copies ran while one was open for 7% -> 0% of each run, Pallas kernels for 0% -> 0%
where the time goes in v1:
time: 33.4 us; the launch traced here: 33.1 us
  Pallas kernels  25.6 us (77%)
  local copies, waits for them, and re-layouts  5.59 us (17%)
  between operations  1.94 us (6%)
    pallas_call x1, Pallas kernels, body(): pl.pallas_call(functools.partial(kernel, n, ring), out_shape=(jax.ShapeDt...  25.6 us
    unnamed x10, local copies, waits for them, and re-layouts  5.59 us

profile of v1, /device:TPU:0, one launch (start us, length us, event | category | flops | bytes accessed | tf_op | source)
XLA Modules:
  0.0 33.1 jit_solution(8640975385490173798)
XLA Ops:
  1.9 0.0 copy-start
  1.9 1.6 %copy-done = f32[4,4,4,64,128]{4,3,2,1,0:T(8,128)S(1)} copy-done((f32[4,4,4,64,128]{4,3,2,1,0:T(8,128)S(1)}, f32[4,4,4,64,128]{4,3,2,1,0:T(8,128)}, u32[]{:S(2)}) %copy-start) | copy-done | bytes 2097176
  3.5 0.0 copy-start.1
  3.5 1.0 %copy-done.1 = f32[1,4,4,64,128]{4,3,2,1,0:T(8,128)S(1)} copy-done((f32[1,4,4,64,128]{4,3,2,1,0:T(8,128)S(1)}, f32[1,4,4,64,128]{4,3,2,1,0:T(8,128)}, u32[]{:S(2)}) %copy-start.1) | copy-done | bytes 524312
  4.6 0.0 copy-start.2
  4.6 0.9 %copy-done.2 = f32[4,64,128]{2,1,0:T(8,128)S(1)} copy-done((f32[4,64,128]{2,1,0:T(8,128)S(1)}, f32[4,64,128]{2,1,0:T(8,128)}, u32[]{:S(2)}) %copy-start.2) | copy-done | bytes 131096
  5.5 0.0 copy-start.3
  5.5 0.8 %copy-done.3 = f32[64,128]{1,0:T(8,128)S(1)} copy-done((f32[64,128]{1,0:T(8,128)S(1)}, f32[64,128]{1,0:T(8,128)}, u32[]{:S(2)}) %copy-start.3) | copy-done | bytes 32792
  6.2 25.6 %shard_map.77 = (f32[1,4,4,64,128]{4,3,2,1,0:T(8,128)S(1)}, f32[1,2]{1,0:T(1,128)S(1)}) custom-call(s32[1]{0:T(128)S(6)} %copy.10.anc_ref, s32[1]{0:T(128)S(6)} %copy.11.sel_ref, f32[1,4,4,64,128]{4,3,2,1,0:T(8,128)S(1)} %copy-done.1, f32[4,4,4,64,128]{4,3,2,1,0:T(8,128)S(1)} %copy-done, f32[4,64,128]{2,1,0:T(8,128)S(1)} %copy-done.2, f32[64,128]{1,0:T(8,128)S(1)} %copy-done.3), custom_call_target="tpu_custom_call" | custom-call | tf_op jit(solution)/shard_map/pallas_call | solution.py:345
  31.8 0.8 %copy.12 = f32[1,4,4,64,128]{4,3,2,1,0:T(8,128)} copy(f32[1,4,4,64,128]{4,3,2,1,0:T(8,128)S(1)} %get-tuple-element.4) | data formatting | bytes 1048576
  32.6 0.5 %copy.13 = f32[1,2]{1,0:T(1,128)} copy(f32[1,2]{1,0:T(1,128)S(1)} %get-tuple-element.5) | data formatting | bytes 16
Async XLA Ops:
  1.9 1.6 %copy-start = (f32[4,4,4,64,128]{4,3,2,1,0:T(8,128)S(1)}, f32[4,4,4,64,128]{4,3,2,1,0:T(8,128)}, u32[]{:S(2)}) copy-start(f32[4,4,4,64,128]{4,3,2,1,0:T(8,128)} %pert_ref.1) | copy-start | bytes 6291460
  3.5 1.0 %copy-start.1 = (f32[1,4,4,64,128]{4,3,2,1,0:T(8,128)S(1)}, f32[1,4,4,64,128]{4,3,2,1,0:T(8,128)}, u32[]{:S(2)}) copy-start(f32[1,4,4,64,128]{4,3,2,1,0:T(8,128)} %init_ref.1) | copy-start | bytes 1572868
  4.6 0.9 %copy-start.2 = (f32[4,64,128]{2,1,0:T(8,128)S(1)}, f32[4,64,128]{2,1,0:T(8,128)}, u32[]{:S(2)}) copy-start(f32[4,64,128]{2,1,0:T(8,128)} %kap_ref.1) | copy-start | bytes 393220
  5.5 0.8 %copy-start.3 = (f32[64,128]{1,0:T(8,128)S(1)}, f32[64,128]{1,0:T(8,128)}, u32[]{:S(2)}) copy-start(f32[64,128]{1,0:T(8,128)} %weight_ref.1) | copy-start | bytes 98308

commit v2 on v1

--- a/solution.py
+++ b/solution.py
@@ -10,13 +10,15 @@
 STEPS = 3
 TIME_STEP = 0.2
 EDGE = 8
+VMEM_LIMIT = 66000000
 MESH_ID = pl.DeviceIdType.MESH
 
 
 def kernel(
-    n, ring, anc_ref, sel_ref, init_ref, pert_ref, kap_ref, weight_ref, out_ref, act_ref,
+    n, ring, anc_hbm, sel_hbm, init_ref, pert_ref, kap_ref, weight_ref, out_ref, act_ref,
     full, state, own, pert, pert_edge, pert_halo, edge, kap, face, coef, weight, part,
     x_send, x_recv, p_send, p_recv, z_send, z_recv, s_send, s_recv, local_sem,
+    token, anc_ref, sel_ref,
 ):
     _, fields, levels, width, lat = init_ref.shape
     rows = width + 2 * EDGE
@@ -36,37 +38,54 @@
         pltpu.make_async_copy(kap_ref, kap.at[:, pl.ds(EDGE, width)], local_sem.at[2]),
         pltpu.make_async_copy(weight_ref, weight, local_sem.at[3]),
         pltpu.make_async_copy(pert_ref, pert, local_sem.at[4]),
+        pltpu.make_async_copy(anc_hbm, anc_ref, local_sem.at[5]),
+        pltpu.make_async_copy(sel_hbm, sel_ref, local_sem.at[6]),
     ]
     for copy in local:
         copy.start()
 
     barrier = pltpu.get_barrier_semaphore()
-    peers = 0
     for k in range(1, groups):
         pl.semaphore_signal(
             barrier, inc=1, device_id={"mem": lax.rem(mem + 2 * k, n)}, device_id_type=MESH_ID
         )
-        peers += 1
     pl.semaphore_signal(barrier, inc=1, device_id={"mem": twin}, device_id_type=MESH_ID)
-    peers += 1
-    for d in range(1, ring):
-        pl.semaphore_signal(
-            barrier, inc=1, device_id={"lon": lax.rem(lon + d, ring)}, device_id_type=MESH_ID
-        )
-        peers += 1
-    pl.semaphore_wait(barrier, peers)
+
+    def toward(semaphore, up):
+        @pl.when(lon < ring - 1 if up else lon > 0)
+        def _():
+            pl.semaphore_signal(
+                semaphore, inc=1, device_id={"lon": east if up else west}, device_id_type=MESH_ID
+            )
+
+    toward(barrier, True)
+    toward(barrier, False)
+    beside = jnp.where(lon > 0, 1, 0) + jnp.where(lon < ring - 1, 1, 0)
+    pl.semaphore_wait(barrier, groups + beside)
+
+    def pass_token(up):
+        @pl.when(lon > 0 if up else lon < ring - 1)
+        def _():
+            pl.semaphore_wait(token.at[int(up)], 1)
+
+        toward(token.at[int(up)], up)
 
     def view(block, kind, level):
         if kind == "lo":
-            return block.at[:, :, pl.ds(0, EDGE)]
+            return block.at[pl.ds(0, dyn), :, pl.ds(0, EDGE)]
         if kind == "hi":
-            return block.at[:, :, pl.ds(top, EDGE)]
+            return block.at[pl.ds(0, dyn), :, pl.ds(top, EDGE)]
+        if kind == "hum_lo":
+            return block.at[dyn, :, pl.ds(0, EDGE)]
+        if kind == "hum_hi":
+            return block.at[dyn, :, pl.ds(top, EDGE)]
         if kind == "dyn":
             return block.at[pl.ds(0, dyn), level, pl.ds(EDGE, width - 2 * EDGE)]
         return block.at[dyn, level, pl.ds(EDGE, width - 2 * EDGE)]
 
     def sem_of(kind, level):
-        return {"lo": 0, "hi": 1, "dyn": 2 + level, "hum": 2 + levels + level}[kind]
+        base = {"lo": 0, "hi": 1, "hum_lo": 2, "hum_hi": 3, "dyn": 4, "hum": 4 + levels}
+        return base[kind] + level
 
     def across(k, kind, level):
         slot = sem_of(kind, level)
@@ -104,12 +123,25 @@
 
     low, high = pl.ds(0, EDGE), pl.ds(EDGE + width, EDGE)
     first, last = pl.ds(0, EDGE), pl.ds(top, EDGE)
-    pieces = [("lo", 0), ("hi", 0)]
+    pieces = [("lo", 0), ("hi", 0), ("hum_lo", 0), ("hum_hi", 0)]
     pieces += [("dyn", level) for level in range(levels)]
     pieces += [("hum", level) for level in range(levels)]
     for kind, level in pieces:
         for k in range(1, groups):
             across(k, kind, level).start()
+    for kind, level in pieces:
+        to_twin(0, kind, level).start()
+
+    @pl.when(2 * lon < ring)
+    def _():
+        pass_token(True)
+        pass_token(False)
+
+    @pl.when(2 * lon >= ring)
+    def _():
+        pass_token(False)
+        pass_token(True)
+
     own_halo = [
         lon_copy(init_ref.at[0, pl.ds(0, dyn), :, first], own.at[:, :, high], 0, 0),
         lon_copy(init_ref.at[0, pl.ds(0, dyn), :, last], own.at[:, :, low], 0, 1),
@@ -118,28 +150,30 @@
         lon_copy(kap_ref.at[:, first], kap.at[:, high], 1, 0),
         lon_copy(kap_ref.at[:, last], kap.at[:, low], 1, 1),
     ]
-    for copy in kap_halo + own_halo:
-        copy.start()
-    for kind, level in pieces:
-        to_twin(0, kind, level).start()
-
-    local[4].wait()
+    for copy in kap_halo:
+        copy.start()
+
+    for copy in local:
+        copy.wait()
     chosen = sel_ref[0]
-    for f in range(fields):
-        for level in range(levels):
-            pert_edge[0, f, level] = pert[chosen, f, level, 0:EDGE, :]
-            pert_edge[1, f, level] = pert[chosen, f, level, top:width, :]
+    packed = pert_edge.shape[2]
+    for level in range(levels):
+        for f in range(fields):
+            spot = pl.ds(f * STEPS, STEPS)
+            pert_edge[0, level, spot, :] = pert[chosen, f, level, 0:STEPS, :]
+            pert_edge[1, level, spot, :] = pert[chosen, f, level, width - STEPS : width, :]
+        if packed > fields * STEPS:
+            rest = packed - fields * STEPS
+            for side in range(2):
+                pert_edge[side, level, pl.ds(fields * STEPS, rest), :] = jnp.zeros(
+                    (rest, lat), jnp.float32
+                )
     pert_copy = [
         lon_copy(pert_edge.at[0], pert_halo.at[1], 2, 0),
         lon_copy(pert_edge.at[1], pert_halo.at[0], 2, 1),
     ]
     for copy in pert_copy:
         copy.start()
-
-    for copy in local[:4]:
-        copy.wait()
-    for copy in kap_halo:
-        copy.wait()
 
     lane = lax.broadcasted_iota(jnp.int32, (rows, lat), 1)
     not_north = jnp.where(lane == lat - 1, 0.0, 1.0)
@@ -167,8 +201,6 @@
         face[3, level] = from_south(to_north)
         return 0
 
-    lax.fori_loop(0, levels, faces, 0)
-
     def coefficients(u, v, level):
         u = TIME_STEP * u
         v = TIME_STEP * v
@@ -191,9 +223,6 @@
         inner = t[EDGE : EDGE + width, :]
         terms = weight[...] * inner * inner
         return jnp.sum(terms.reshape(width // 8, 8, lat), axis=0)
-
-    for copy in own_halo:
-        copy.wait()
 
     def own_level(level, total):
         u, v, t = own[0, level], own[1, level], own[2, level]
@@ -205,8 +234,6 @@
             t = t_next
             total = total + observed(t)
         return total
-
-    part[0, lon] = lax.fori_loop(0, levels, own_level, jnp.zeros((8, lat), jnp.float32))
 
     def share(which):
         return [
@@ -232,9 +259,6 @@
 
     arrive("lo", 0)
     arrive("hi", 0)
-    first_share = share(0)
-    for copy in first_share:
-        copy.start()
     settled("lo", 0)
     settled("hi", 0)
     ancestor = anc_ref[0]
@@ -245,7 +269,7 @@
             value = jnp.where(ancestor == j, load(j), value)
         return value
 
-    for f in range(fields):
+    def pick_edges(f):
         for level in range(levels):
             lower = pick(lambda j: full[j, f, level, 0:EDGE, :])
             upper = pick(lambda j: full[j, f, level, top:width, :])
@@ -253,13 +277,33 @@
             edge[1, f, level] = upper
             state[f, level, EDGE : 2 * EDGE, :] = lower
             state[f, level, width : width + EDGE, :] = upper
-    edge_copy = [
-        lon_copy(edge.at[0], state.at[:, :, high], 3, 0),
-        lon_copy(edge.at[1], state.at[:, :, low], 3, 1),
-    ]
+
+    def pass_edges(fs, slot):
+        return [
+            lon_copy(edge.at[0, fs], state.at[fs, :, high], slot, 0),
+            lon_copy(edge.at[1, fs], state.at[fs, :, low], slot, 1),
+        ]
+
+    for f in range(dyn):
+        pick_edges(f)
+    edge_copy = pass_edges(pl.ds(0, dyn), 3)
     for copy in edge_copy:
         copy.start()
-    arrive("dyn", 0)
+    arrive("hum_lo", 0)
+    arrive("hum_hi", 0)
+    settled("hum_lo", 0)
+    settled("hum_hi", 0)
+    pick_edges(dyn)
+    hum_edge_copy = pass_edges(dyn, 4)
+    for copy in hum_edge_copy + own_halo:
+        copy.start()
+    for copy in kap_halo:
+        copy.wait()
+    lax.fori_loop(0, levels, faces, 0)
+    first_share = share(0)
+
+    for level in range(levels - 2):
+        arrive("dyn", level)
     for copy in pert_copy + edge_copy:
         copy.wait()
 
@@ -270,19 +314,12 @@
         return state[f, level]
 
     def noise(f, level):
-        return jnp.concatenate(
-            [pert_halo[0, f, level], pert[chosen, f, level], pert_halo[1, f, level]], axis=0
-        )
+        spot = slice(f * STEPS, (f + 1) * STEPS)
+        blank = jnp.zeros((EDGE - STEPS, lat), jnp.float32)
+        lower, upper = pert_halo[0, level, spot, :], pert_halo[1, level, spot, :]
+        return jnp.concatenate([blank, lower, pert[chosen, f, level], upper, blank], axis=0)
 
     def dyn_level(level, total):
-        @pl.when(level < levels - 1)
-        def _():
-            arrive("dyn", level + 1)
-
-        @pl.when(level == levels - 1)
-        def _():
-            arrive("hum", 0)
-
         settled("dyn", level)
         u, v, t = fill(0, level), fill(1, level), fill(2, level)
         for step in range(2 * STEPS):
@@ -298,6 +335,23 @@
         out_ref[0, 0, level] = u[inner]
         out_ref[0, 1, level] = v[inner]
         out_ref[0, 2, level] = t[inner]
+
+        @pl.when(level == 0)
+        def _():
+            arrive("dyn", levels - 2)
+
+        @pl.when(level == levels - 2)
+        def _():
+            arrive("dyn", levels - 1)
+            for copy in own_halo:
+                copy.wait()
+            part[0, lon] = lax.fori_loop(
+                0, levels, own_level, jnp.zeros((8, lat), jnp.float32)
+            )
+            for copy in first_share:
+                copy.start()
+            arrive("hum", 0)
+
         return total
 
     part[1, lon] = lax.fori_loop(0, levels, dyn_level, jnp.zeros((8, lat), jnp.float32))
@@ -305,10 +359,14 @@
     for copy in second_share:
         copy.start()
 
+    arrive("hum", 1)
+    for copy in hum_edge_copy:
+        copy.wait()
+
     def hum_level(level, carry):
-        @pl.when(level < levels - 1)
+        @pl.when(level < levels - 2)
         def _():
-            arrive("hum", level + 1)
+            arrive("hum", level + 2)
 
         settled("hum", level)
         q = fill(dyn, level)
@@ -322,10 +380,13 @@
     lax.fori_loop(0, levels, hum_level, 0)
 
     cells = levels * lat * width * ring
+    action = []
     for which, copies in enumerate((first_share, second_share)):
         for copy in copies:
             copy.wait()
-        act_ref[0, which] = jnp.sum(jnp.sum(part[which], axis=0)) / cells
+        action.append(jnp.sum(jnp.sum(part[which], axis=0)) / cells)
+    column = lax.broadcasted_iota(jnp.int32, (1, 2), 1)
+    act_ref[...] = jnp.where(column == 0, action[0], action[1])
     for kind, level in pieces:
         for k in range(1, groups):
             across(k, kind, level).wait_send()
@@ -337,26 +398,26 @@
     n, ring = lax.axis_size("mem"), lax.axis_size("lon")
     _, fields, levels, width, lat = initial_state.shape
     rows = width + 2 * EDGE
-    kinds = 2 + 2 * levels
+    kinds = 4 + 2 * levels
+    packed = -(-fields * STEPS // 8) * 8
     f32 = jnp.float32
-    any_space = pl.BlockSpec(memory_space=pl.ANY)
-    smem = pl.BlockSpec(memory_space=pltpu.SMEM)
+    any_space = pl.BlockSpec(memory_space=pltpu.HBM)
     dma = pltpu.SemaphoreType.DMA
     return pl.pallas_call(
         functools.partial(kernel, n, ring),
         out_shape=(
-            jax.ShapeDtypeStruct(initial_state.shape, f32),
-            jax.ShapeDtypeStruct((1, 2), f32),
+            pltpu.VMEM(initial_state.shape, f32),
+            pltpu.VMEM((1, 2), f32),
         ),
-        in_specs=[smem, smem, any_space, any_space, any_space, any_space],
-        out_specs=(pl.BlockSpec(memory_space=pltpu.VMEM), smem),
+        in_specs=[any_space] * 6,
+        out_specs=(pl.BlockSpec(memory_space=pltpu.VMEM),) * 2,
         scratch_shapes=[
             pltpu.VMEM((n, fields, levels, width, lat), f32),
             pltpu.VMEM((fields, levels, rows, lat), f32),
             pltpu.VMEM((fields - 1, levels, rows, lat), f32),
             pltpu.VMEM(perturbations.shape, f32),
-            pltpu.VMEM((2, fields, levels, EDGE, lat), f32),
-            pltpu.VMEM((2, fields, levels, EDGE, lat), f32),
+            pltpu.VMEM((2, levels, packed, lat), f32),
+            pltpu.VMEM((2, levels, packed, lat), f32),
             pltpu.VMEM((2, fields, levels, EDGE, lat), f32),
             pltpu.VMEM((levels, rows, lat), f32),
             pltpu.VMEM((4, levels, rows, lat), f32),
@@ -367,14 +428,17 @@
             dma((n // 2 - 1, kinds)),
             dma((n // 2, kinds)),
             dma((n // 2, kinds)),
-            dma((4, 2)),
-            dma((4, 2)),
+            dma((5, 2)),
+            dma((5, 2)),
             dma((2, ring - 1)),
             dma((2, ring - 1)),
-            dma((5,)),
+            dma((7,)),
+            pltpu.SemaphoreType.REGULAR((2,)),
+            pltpu.SMEM((1,), jnp.int32),
+            pltpu.SMEM((1,), jnp.int32),
         ],
         compiler_params=pltpu.CompilerParams(
-            collective_id=0, has_side_effects=True, vmem_limit_bytes=40 * 1024 * 1024
+            collective_id=0, has_side_effects=True, vmem_limit_bytes=VMEM_LIMIT
         ),
     )(ancestor, selector, initial_state, perturbations, diffusivity, region_weight)
 

time: 33.4 us -> 26.7 us (0.80)
  local copies, waits for them, and re-layouts: 5.59 us -> 1.31 us
  Pallas kernels: 25.6 us -> 23.3 us
    unnamed x10 -> x2, local copies, waits for them, and re-layouts: 5.59 us -> 1.31 us
    pallas_call x1, Pallas kernels: 25.6 us -> 23.3 us  [body(): pl.pallas_call(functools.partial(kernel, n, ring), out_shape=(pltpu.VMEM(...]
where the time goes in v2:
time: 26.7 us; the launch traced here: 26.6 us
  Pallas kernels  23.3 us (87%)
  between operations  1.93 us (7%)
  local copies, waits for them, and re-layouts  1.31 us (5%)
    pallas_call x1, Pallas kernels, body(): pl.pallas_call(functools.partial(kernel, n, ring), out_shape=(pltpu.VMEM(...  23.3 us
    unnamed x2, local copies, waits for them, and re-layouts  1.31 us

profile of v2, /device:TPU:0, one launch (start us, length us, event | category | flops | bytes accessed | tf_op | source)
XLA Modules:
  0.0 26.6 jit_solution(9310460590600537065)
XLA Ops:
  1.9 23.3 %shard_map.77 = (f32[1,4,4,64,128]{4,3,2,1,0:T(8,128)S(1)}, f32[1,2]{1,0:T(1,128)S(1)}) custom-call(s32[1]{0:T(128)S(6)} %copy.12.anc_hbm, s32[1]{0:T(128)S(6)} %copy.13.sel_hbm, f32[1,4,4,64,128]{4,3,2,1,0:T(8,128)} %init_ref.1, f32[4,4,4,64,128]{4,3,2,1,0:T(8,128)} %pert_ref.1, f32[4,64,128]{2,1,0:T(8,128)} %kap_ref.1, f32[64,128]{1,0:T(8,128)} %weight_ref.1), custom_call_target="tpu_custom_call" | custom-call | tf_op jit(solution)/shard_map/pallas_call | solution.py:406
  25.3 0.8 %copy.10 = f32[1,4,4,64,128]{4,3,2,1,0:T(8,128)} copy(f32[1,4,4,64,128]{4,3,2,1,0:T(8,128)S(1)} %get-tuple-element.2) | data formatting | bytes 1048576
  26.1 0.5 %copy.11 = f32[1,2]{1,0:T(1,128)} copy(f32[1,2]{1,0:T(1,128)S(1)} %get-tuple-element.3) | data formatting | bytes 16

commit v3 on v2

--- a/solution.py
+++ b/solution.py
@@ -129,19 +129,6 @@
     for kind, level in pieces:
         for k in range(1, groups):
             across(k, kind, level).start()
-    for kind, level in pieces:
-        to_twin(0, kind, level).start()
-
-    @pl.when(2 * lon < ring)
-    def _():
-        pass_token(True)
-        pass_token(False)
-
-    @pl.when(2 * lon >= ring)
-    def _():
-        pass_token(False)
-        pass_token(True)
-
     own_halo = [
         lon_copy(init_ref.at[0, pl.ds(0, dyn), :, first], own.at[:, :, high], 0, 0),
         lon_copy(init_ref.at[0, pl.ds(0, dyn), :, last], own.at[:, :, low], 0, 1),
@@ -150,8 +137,30 @@
         lon_copy(kap_ref.at[:, first], kap.at[:, high], 1, 0),
         lon_copy(kap_ref.at[:, last], kap.at[:, low], 1, 1),
     ]
-    for copy in kap_halo:
-        copy.start()
+
+    def start_halo(near):
+        for side, inside in enumerate((lon > 0, lon < ring - 1)):
+
+            @pl.when(inside if near else jnp.logical_not(inside))
+            def _():
+                kap_halo[side].start()
+                own_halo[side].start()
+
+    start_halo(True)
+    for kind, level in pieces:
+        to_twin(0, kind, level).start()
+
+    @pl.when(2 * lon < ring)
+    def _():
+        pass_token(True)
+        pass_token(False)
+
+    @pl.when(2 * lon >= ring)
+    def _():
+        pass_token(False)
+        pass_token(True)
+
+    start_halo(False)
 
     for copy in local:
         copy.wait()
@@ -295,12 +304,16 @@
     settled("hum_hi", 0)
     pick_edges(dyn)
     hum_edge_copy = pass_edges(dyn, 4)
-    for copy in hum_edge_copy + own_halo:
-        copy.start()
-    for copy in kap_halo:
+    for copy in hum_edge_copy:
+        copy.start()
+
+    for copy in kap_halo + own_halo:
         copy.wait()
     lax.fori_loop(0, levels, faces, 0)
+    part[0, lon] = lax.fori_loop(0, levels, own_level, jnp.zeros((8, lat), jnp.float32))
     first_share = share(0)
+    for copy in first_share:
+        copy.start()
 
     for level in range(levels - 2):
         arrive("dyn", level)
@@ -343,13 +356,6 @@
         @pl.when(level == levels - 2)
         def _():
             arrive("dyn", levels - 1)
-            for copy in own_halo:
-                copy.wait()
-            part[0, lon] = lax.fori_loop(
-                0, levels, own_level, jnp.zeros((8, lat), jnp.float32)
-            )
-            for copy in first_share:
-                copy.start()
             arrive("hum", 0)
 
         return total

time: 26.7 us -> 26.7 us (level)
  no operation moved by 1% of the time
where the time goes in v3:
time: 26.7 us; the launch traced here: 26.5 us
  Pallas kernels  23.3 us (87%)
  between operations  1.93 us (7%)
  local copies, waits for them, and re-layouts  1.31 us (5%)
    pallas_call x1, Pallas kernels, body(): pl.pallas_call(functools.partial(kernel, n, ring), out_shape=(pltpu.VMEM(...  23.3 us
    unnamed x2, local copies, waits for them, and re-layouts  1.31 us

profile of v3, /device:TPU:0, one launch (start us, length us, event | category | flops | bytes accessed | tf_op | source)
XLA Modules:
  0.0 26.5 jit_solution(1041134722582416438)
XLA Ops:
  1.9 23.3 %shard_map.77 = (f32[1,4,4,64,128]{4,3,2,1,0:T(8,128)S(1)}, f32[1,2]{1,0:T(1,128)S(1)}) custom-call(s32[1]{0:T(128)S(6)} %copy.12.anc_hbm, s32[1]{0:T(128)S(6)} %copy.13.sel_hbm, f32[1,4,4,64,128]{4,3,2,1,0:T(8,128)} %init_ref.1, f32[4,4,4,64,128]{4,3,2,1,0:T(8,128)} %pert_ref.1, f32[4,64,128]{2,1,0:T(8,128)} %kap_ref.1, f32[64,128]{1,0:T(8,128)} %weight_ref.1), custom_call_target="tpu_custom_call" | custom-call | tf_op jit(solution)/shard_map/pallas_call | solution.py:412
  25.2 0.8 %copy.10 = f32[1,4,4,64,128]{4,3,2,1,0:T(8,128)} copy(f32[1,4,4,64,128]{4,3,2,1,0:T(8,128)S(1)} %get-tuple-element.2) | data formatting | bytes 1048576
  26.0 0.5 %copy.11 = f32[1,2]{1,0:T(1,128)} copy(f32[1,2]{1,0:T(1,128)S(1)} %get-tuple-element.3) | data formatting | bytes 16
